TPU v7x, 128 devices: a whole 4x4x4 slice. The times are simulated.
128 devices in a mesh: dom: 64 (over x, z, y), sub: 2 (over core).
Axes of the slice: x: 4, y: 4, z: 4, core: 2. Of those that a mesh axis runs over, the one named last changes fastest.
Arguments:
- a_blocks: bfloat16 [8192, 8, 128, 128], P(('dom', 'sub')), may hold values from -6 to 6
- nbr_offset: int32 [8192, 8], P(('dom', 'sub')), may hold values from -3 to 3
- nbr_count: int32 [8192], P(('dom', 'sub')), may hold values from 4 to 8
- prolong: bfloat16 [8192, 128, 128], P(('dom', 'sub')), may hold values from -0.5 to 0.5
- owner_start: int32 [128], replicated, may hold values from 0 to 8191, as said below
Outputs:
- coarse: float32 [2048, 7, 128, 128], P(('dom', 'sub'))
Inputs may be any that keep to these rules, and one draw needn't show every extreme that they name: owner_start[0] = 0, owner_start[1] = 112, and owner_start[d] - d * 64 lies in 0 to 48 for every d.
All inputs are finite; a program needn't handle non-finite values.
Results may differ from a plain program's by a relative error of at most 0.0029.
Values may be sent and summed in bfloat16 or wider, within the bound.
A program may use at most 256 MiB of HBM per device.

v0:
```python
import functools

import jax
import jax.numpy as jnp
from jax import lax
from jax.experimental import pallas as pl
from jax.experimental.pallas import tpu as pltpu
from jax.sharding import PartitionSpec as P

BF = jnp.bfloat16
F32 = jnp.float32
W = 3
KC = 7
AD = 16
K = 8
B = 128
RB = 64
CHUNKS = (21, 24)
LAST_ROW = 24
FIRST_ROWS = 20
GROUP = 4
PAD = 7
OWN = AD * KC
SPARE = KC


def bases():
    at, out = OWN + PAD, []
    for size in CHUNKS:
        out.append(at)
        at += size + 2 * PAD
    return out, at


BASES, TRASH = bases()
CLEAR = 8
BLOCKS = -(-(TRASH + KC) // CLEAR) * CLEAR

T_GOAL = K
T_HEAD = K + 1
T_PHASE = K + 2
T_RECV = K + 3
TABLE = (16, 128)
EARLY = 48
VMEM_LIMIT = 8 << 20


class Frame:
    def __init__(self, starts, dev, devices):
        def start_of(d):
            inner = starts[jnp.clip(d, 0, devices - 1)]
            return jnp.where(d >= devices, devices * RB, inner) - dev * RB

        self.initial = dev == 0
        self.final = dev >= devices - 1
        self.begin = [start_of(jnp.maximum(dev - 1, 0)), start_of(dev), start_of(dev + 1)]
        ends = [self.begin[1], self.begin[2], start_of(dev + 2)]
        self.length = [jnp.maximum(e - b, 1) for b, e in zip(self.begin, ends)]
        self.shift = jnp.where(dev >= devices, 0, self.begin[1])
        self.scale = [lax.div(jnp.int32(1 << 20), n) + 1 for n in self.length]

    def agg_start(self, owner, a):
        return self.begin[owner] + lax.shift_right_arithmetic(a * self.length[owner] + (AD - 1), 4)

    def agg(self, i):
        p0, p1, p2 = [i - b for b in self.begin]
        later = jnp.logical_or(p1 >= 0, self.initial)
        last = jnp.logical_and(p2 >= 0, jnp.logical_not(self.final))
        p = jnp.where(last, p2, jnp.where(later, p1, p0))
        m = jnp.where(last, self.scale[2], jnp.where(later, self.scale[1], self.scale[0]))
        o = jnp.where(last, 2 * AD, jnp.where(later, AD, 0))
        a = lax.shift_right_arithmetic(jnp.maximum(p, 0) * AD * m, 20)
        return o + jnp.minimum(a, AD - 1)

    def chunks(self):
        second, used, cut = jnp.int32(0), jnp.int32(0), jnp.int32(-1)
        found = []
        for a in range(AD):
            i0 = jnp.maximum(self.agg_start(0, a), 0)
            i1 = self.agg_start(0, a + 1)
            here = jnp.logical_and(i1 > 0, self.shift > 0)
            low = self.agg(i0 - W) - a + W
            n = jnp.where(here, self.agg(i1 + W - 1) - a + W - low + 1, 0)
            full = jnp.logical_or(used + n > CHUNKS[0], i0 >= LAST_ROW)
            over = jnp.logical_and(jnp.logical_and(second == 0, full), here)
            cut = jnp.where(over, i0, cut)
            place = jnp.where(over, 0, used)
            second = jnp.where(over, 1, second)
            found.append((second, place, low, n))
            used = place + n
        return found, cut

    def boundary(self, target, limit=RB):
        row, before = jnp.int32(RB), jnp.int32(AD)
        for a in range(AD, -1, -1):
            start = self.agg_start(1, a)
            take = jnp.logical_or(start >= target, row > limit)
            row, before = jnp.where(take, start, row), jnp.where(take, a, before)
        return jnp.minimum(row, RB), before


def position():
    return lax.axis_index("dom") * lax.axis_size("sub") + lax.axis_index("sub")


def total():
    return lax.axis_size("dom") * lax.axis_size("sub")


def fill_table(starts, offs, counts, tab):
    dev, devices = position(), total()
    lane = lax.broadcasted_iota(jnp.int32, (1, 128), 1)

    def lanes(values):
        out = jnp.zeros((1, 128), jnp.int32)
        for n, value in enumerate(values):
            out = jnp.where(lane == n, value, out)
        return out

    arriving, _ = Frame(starts, dev + 1, devices).chunks()
    tab[T_RECV : T_RECV + 1] = lanes(
        [((second * 64 + place) * 16 + low) * 16 + n for second, place, low, n in arriving]
    )

    frame = Frame(starts, dev, devices)
    leaving, cut = frame.chunks()

    own_cut, own_cut_a = frame.boundary(jnp.maximum(frame.shift, FIRST_ROWS))
    r1 = jnp.where(cut >= 0, cut, own_cut)
    r1_a = jnp.where(cut >= 0, 0, own_cut_a)
    e1, e1_a = frame.boundary(jnp.maximum(frame.shift, r1 + FIRST_ROWS), EARLY)
    tab[T_PHASE : T_PHASE + 1] = lanes([r1, e1, r1_a, e1_a, 0, r1, 0, r1_a, e1, RB, e1_a, AD])

    i = lane[:, :RB]
    a = frame.agg(i)
    first = frame.agg(i - W) - a + W
    slots = frame.agg(i + W) - a + W - first + 1
    goal = jnp.maximum(a - AD, 0) * KC
    for n, (second, place, low, count) in enumerate(leaving):
        block = jnp.where(second == 1, BASES[1], BASES[0]) + place - low
        goal = jnp.where(a == n, block, goal)
    tab[T_GOAL : T_GOAL + 1, :RB] = goal
    tab[T_HEAD : T_HEAD + 1, :RB] = first + 16 * slots + 256 * jnp.maximum(a - AD, 0)

    j_low = jnp.where(dev == 0, 0, -W)
    j_high = jnp.where(dev == devices - 1, RB, RB + W)
    k = lax.broadcasted_iota(jnp.int32, (K, RB), 0)
    j = lax.broadcasted_iota(jnp.int32, (K, RB), 1) + offs[...]
    ok = jnp.logical_and(k < counts[...], jnp.logical_and(j >= j_low, j < j_high))
    slot = jnp.where(ok, frame.agg(j) - a + W, SPARE)
    tab[:K, :RB] = slot * 256 + j + W


def edges_kernel(
    starts_hbm, offs_hbm, counts_hbm, a_hbm, p_hbm, av, win, blocks, tab,
    starts, offs, counts, send, recv, a_sems, sems,
):
    small = [
        pltpu.make_async_copy(src, dst, sems.at[n])
        for n, (src, dst) in enumerate(
            ((starts_hbm, starts), (offs_hbm, offs), (counts_hbm, counts))
        )
    ]
    parts = a_sems.shape[0]
    size = EARLY // parts
    local = [pltpu.make_async_copy(p_hbm, win.at[pl.ds(W, RB)], sems.at[3])]
    for n in range(parts):
        rows = pl.ds(n * size, size)
        local.append(pltpu.make_async_copy(a_hbm.at[rows], av.at[rows], a_sems.at[n]))

    dev, devices = position(), total()
    cores = lax.axis_size("sub")

    def device(d):
        d = lax.rem(d + devices, devices)
        return (lax.div(d, cores), lax.rem(d, cores))

    left, right = device(dev - 1), device(dev + 1)
    mesh = pl.DeviceIdType.MESH
    barrier = pltpu.get_barrier_semaphore()
    for other in (left, right):
        pl.semaphore_signal(barrier, inc=1, device_id=other, device_id_type=mesh)
    for copy in small + local:
        copy.start()

    for copy in small:
        copy.wait()
    fill_table(starts, offs, counts, tab)

    pl.semaphore_wait(barrier, 2)
    copies = [
        pltpu.make_async_remote_copy(
            src_ref=p_hbm.at[pl.ds(src, W)],
            dst_ref=win.at[pl.ds(dst, W)],
            send_sem=send.at[n],
            recv_sem=recv.at[n],
            device_id=other,
            device_id_type=mesh,
        )
        for n, src, dst, other in ((0, RB - W, 0, right), (1, 0, RB + W, left))
    ]
    for copy in copies:
        copy.start()

    def clear(b, carry):
        for n in range(CLEAR):
            blocks[b * CLEAR + n] = jnp.zeros((B, B), F32)
        return carry

    lax.fori_loop(0, BLOCKS // CLEAR, clear, 0)
    for copy in local + copies:
        copy.wait()


def edges_call(starts, offs, counts, a, p):
    vmem = pl.BlockSpec(memory_space=pltpu.VMEM)
    hbm = pl.BlockSpec(memory_space=pltpu.HBM)
    return pl.pallas_call(
        edges_kernel,
        out_shape=[
            jax.ShapeDtypeStruct((RB, K, B, B), BF),
            jax.ShapeDtypeStruct((RB + 2 * W, B, B), BF),
            jax.ShapeDtypeStruct((BLOCKS, B, B), F32),
            jax.ShapeDtypeStruct(TABLE, jnp.int32),
        ],
        in_specs=[hbm] * 5,
        out_specs=[vmem] * 4,
        scratch_shapes=[
            pltpu.SMEM(starts.shape, jnp.int32),
            pltpu.VMEM(offs.shape, jnp.int32),
            pltpu.VMEM(counts.shape, jnp.int32),
            pltpu.SemaphoreType.DMA((2,)),
            pltpu.SemaphoreType.DMA((2,)),
            pltpu.SemaphoreType.DMA((4,)),
            pltpu.SemaphoreType.DMA((4,)),
        ],
        compiler_params=pltpu.CompilerParams(
            collective_id=0, has_side_effects=True, vmem_limit_bytes=VMEM_LIMIT
        ),
        cost_estimate=pl.CostEstimate(flops=1000, bytes_accessed=20 << 20, transcendentals=0),
        name="edges",
    )(starts, offs, counts, a, p)


def received(tab, a):
    v = tab[T_RECV, a]
    n = jnp.bitwise_and(v, 15)
    low = jnp.bitwise_and(lax.shift_right_logical(v, 4), 15)
    place = jnp.bitwise_and(lax.shift_right_logical(v, 8), 63)
    return lax.shift_right_logical(v, 14), place, low, n


def phase_kernel(phase, *refs):
    refs = list(refs)
    tab_in, win, state, av = refs[:4]
    del refs[:4]
    a_hbm = refs.pop(0) if phase == 0 else None
    arrived = refs.pop(0) if phase == 2 else None
    blocks = refs.pop(0)
    extra = refs.pop(0)
    if phase == 0:
        av = refs.pop(0)
    out_hbm = refs.pop(0) if phase == 2 else None
    tab, acc, tab_sem, out_sems, late_sem = refs
    del state
    late = pl.ds(EARLY, RB - EARLY)
    if phase == 0:
        late_copy = pltpu.make_async_copy(a_hbm.at[late], av.at[late], late_sem)
        late_copy.start()
    chunk = (1, 0, None)[phase]

    tab_copy = pltpu.make_async_copy(tab_in, tab, tab_sem)
    tab_copy.start()
    tab_copy.wait()
    lo, hi, alo, ahi = [tab[T_PHASE, 4 * phase + n] for n in range(4)]
    rows = hi - lo

    def out_copy(a):
        return pltpu.make_async_copy(
            blocks.at[pl.ds(a * KC, KC)], out_hbm.at[a], out_sems.at[a]
        )

    def put(a, carry):
        out_copy(a).start()
        return carry

    def put_wait(a, carry):
        out_copy(a).wait()
        return carry

    if phase == 2:
        lax.fori_loop(0, alo, put, 0)

        def take(a, carry):
            which, place, low, n = received(tab, a)

            def one(s, carry):
                blocks[a * KC + low + s] = arrived[place + s].astype(F32)
                return carry

            lax.fori_loop(0, jnp.where(which == 1, n, 0), one, 0)
            return carry

        lax.fori_loop(alo, ahi, take, 0)

    def group(g, done):
        places, firsts, goals = [], [], []
        span = jnp.int32(0)
        for u in range(GROUP):
            t = g * GROUP + u
            i = lo + jnp.minimum(t, rows - 1)
            head = tab[T_HEAD, i]
            span = jnp.maximum(span, jnp.bitwise_and(lax.shift_right_logical(head, 4), 15))
            places.append(i)
            firsts.append(jnp.bitwise_and(head, 15))
            goals.append(jnp.where(t < rows, tab[T_GOAL, i], TRASH))

        def compute(slots):
            applied = []
            heads = [jnp.minimum(f, KC - slots) for f in firsts]
            for u in range(GROUP):
                i = places[u]
                for s in range(slots):
                    acc[u, heads[u] + s] = jnp.zeros((B, B), F32)
                for k in range(K):
                    code = tab[k, i]
                    slot = lax.shift_right_logical(code, 8)
                    product = jnp.dot(
                        av[i, k],
                        win[jnp.bitwise_and(code, 255)],
                        preferred_element_type=F32,
                    )
                    acc[u, slot] = acc[u, slot] + product
                applied.append(
                    jnp.concatenate(
                        [acc[u, heads[u] + s].astype(BF) for s in range(slots)], axis=1
                    )
                )
            for u in range(GROUP):
                term = lax.dot_general(
                    win[places[u] + W],
                    applied[u],
                    (((0,), (0,)), ((), ())),
                    preferred_element_type=F32,
                )
                goal = goals[u] + heads[u]
                for s in range(slots):
                    blocks[goal + s] = blocks[goal + s] + term[:, s * B : (s + 1) * B]

        pl.when(span <= 3)(lambda: compute(3))
        pl.when(jnp.logical_and(span > 3, span <= 5))(lambda: compute(5))
        pl.when(span > 5)(lambda: compute(7))

        if phase < 2:
            return done
        t = (g + 1) * GROUP
        ahead = lax.shift_right_logical(tab[T_HEAD, lo + jnp.minimum(t, rows - 1)], 8)
        ready = jnp.where(t < rows, jnp.maximum(ahead, alo), alo)
        return lax.fori_loop(done, jnp.maximum(ready, done), lambda a, c: put(a, c + 1), done)

    done = lax.fori_loop(0, lax.div(rows + (GROUP - 1), GROUP), group, alo)
    if chunk is not None:
        for b in range(CHUNKS[chunk]):
            extra[b] = blocks[BASES[chunk] + b].astype(BF)
        if phase == 0:
            late_copy.wait()
        return
    lax.fori_loop(done, ahi, put, 0)
    part = ahi - 1
    for a in range(AD - 1, -1, -1):
        part = jnp.where(received(tab, a)[3] > 0, a, part)
    for c in range(KC):
        extra[c] = blocks[part * KC + c]
    lax.fori_loop(0, ahi, put_wait, 0)


def phase_call(phase, tab, win, blocks, a, more=()):
    vmem = pl.BlockSpec(memory_space=pltpu.VMEM)
    hbm = pl.BlockSpec(memory_space=pltpu.HBM)
    shapes = [jax.ShapeDtypeStruct((BLOCKS, B, B), F32)]
    in_specs = [vmem] * 4
    out_specs = [vmem, vmem]
    aliases = {2: 0}
    if phase == 2:
        shapes.append(jax.ShapeDtypeStruct((KC, B, B), F32))
        shapes.append(jax.ShapeDtypeStruct((AD, KC, B, B), F32))
        in_specs.append(vmem)
        out_specs.append(hbm)
    else:
        shapes.append(jax.ShapeDtypeStruct((CHUNKS[1 - phase], B, B), BF))
    if phase == 0:
        shapes.append(jax.ShapeDtypeStruct((RB, K, B, B), BF))
        in_specs.append(hbm)
        out_specs.append(vmem)
        aliases[3] = 2
    return pl.pallas_call(
        functools.partial(phase_kernel, phase),
        out_shape=shapes,
        in_specs=in_specs,
        out_specs=out_specs,
        scratch_shapes=[
            pltpu.SMEM(TABLE, jnp.int32),
            pltpu.VMEM((GROUP, K, B, B), F32),
            pltpu.SemaphoreType.DMA,
            pltpu.SemaphoreType.DMA((AD,)),
            pltpu.SemaphoreType.DMA,
        ],
        input_output_aliases=aliases,
        compiler_params=pltpu.CompilerParams(vmem_limit_bytes=VMEM_LIMIT),
        cost_estimate=pl.CostEstimate(
            flops=1_500_000_000, bytes_accessed=8 << 20, transcendentals=0
        ),
        name=f"phase{phase}",
    )(tab, win, blocks, a, *more)


def final_kernel(tab_in, arrived, part, out_in, out_hbm, tab, blocks, sems, tab_sem):
    del out_in
    tab_copy = pltpu.make_async_copy(tab_in, tab, tab_sem)
    tab_copy.start()
    tab_copy.wait()

    def store(a, place, low, s):
        at = place + s
        return pltpu.make_async_copy(blocks.at[at], out_hbm.at[a, low + s], sems.at[at])

    def each(act):
        def visit(a, seen):
            which, place, low, n = received(tab, a)
            n = jnp.where(which == 0, n, 0)

            def one(s, carry):
                act(a, place, low, s, seen)
                return carry

            lax.fori_loop(0, n, one, 0)
            return jnp.where(n > 0, 1, seen)

        lax.fori_loop(0, AD, visit, jnp.int32(0))

    def add(a, place, low, s, seen):
        value = arrived[place + s].astype(F32)
        blocks[place + s] = jnp.where(seen == 0, value + part[low + s], value)
        store(a, place, low, s).start()

    each(add)
    each(lambda a, place, low, s, seen: store(a, place, low, s).wait())


def final_call(tab, arrived, part, out):
    vmem = pl.BlockSpec(memory_space=pltpu.VMEM)
    hbm = pl.BlockSpec(memory_space=pltpu.HBM)
    size = CHUNKS[0]
    return pl.pallas_call(
        final_kernel,
        out_shape=jax.ShapeDtypeStruct((AD, KC, B, B), F32),
        in_specs=[vmem, vmem, vmem, hbm],
        out_specs=hbm,
        scratch_shapes=[
            pltpu.SMEM(TABLE, jnp.int32),
            pltpu.VMEM((size, B, B), F32),
            pltpu.SemaphoreType.DMA((size,)),
            pltpu.SemaphoreType.DMA,
        ],
        input_output_aliases={3: 0},
        compiler_params=pltpu.CompilerParams(vmem_limit_bytes=VMEM_LIMIT),
        cost_estimate=pl.CostEstimate(flops=1_000_000, bytes_accessed=4 << 20, transcendentals=0),
        name="final",
    )(tab, arrived, part, out)


def shards(a_blocks, nbr_offset, nbr_count, prolong, owner_start):
    axes = ("dom", "sub")
    down = [(i + 1, i) for i in range(total() - 1)]
    inputs = (owner_start, nbr_offset.T, nbr_count.reshape(1, RB), a_blocks, prolong)
    inputs = [pltpu.with_memory_space_constraint(x, pltpu.HBM) for x in inputs]
    a, win, blocks, tab = edges_call(*inputs)
    blocks, pack_b, a = phase_call(0, tab, win, blocks, a, inputs[3:4])
    recv_b = lax.ppermute(pack_b, axes, down)
    blocks, pack_a = phase_call(1, tab, win, blocks, a)
    recv_a = lax.ppermute(pack_a, axes, down)
    blocks, part, out = phase_call(2, tab, win, blocks, a, (recv_b,))
    return final_call(tab, recv_a, part, out)


def solution(mesh):
    placed = (
        P(("dom", "sub"), None, None, None),
        P(("dom", "sub"), None),
        P(("dom", "sub")),
        P(("dom", "sub"), None, None),
        P(),
    )
    return jax.shard_map(
        shards,
        mesh=mesh,
        in_specs=placed,
        out_specs=P(("dom", "sub"), None, None, None),
        check_vma=False,
    )
```

profile of v0, /device:TPU:1, one launch (start us, length us, event | category | flops | bytes accessed | tf_op | source)
XLA Modules:
  0.0 44.5 jit_solution(3924136053381311812)
XLA Ops:
  0.0 10.7 %edges.1 = (bf16[64,8,128,128]{3,2,1,0:T(8,128)(2,1)S(1)}, bf16[70,128,128]{2,1,0:T(8,128)(2,1)S(1)}, f32[200,128,128]{2,1,0:T(8,128)S(1)}, s32[16,128]{1,0:T(8,128)S(1)}) custom-call(s32[128]{0:T(128)} %starts_hbm.1, s32[8,64]{1,0:T(8,128)} %bitcast.2, s32[1,64]{1,0:T(1,128)} %bitcast.3, bf16[64,8,128,128]{3,2,1,0:T(8,128)(2,1)} %refs_4_.1, ...), custom_call_target="tpu_custom_call" | custom-call | flops 1000 | bytes 20971520 | tf_op jit(solution)/shard_map/edges/pallas_call | solution.py:218
  10.7 6.1 %phase0.1 = (f32[200,128,128]{2,1,0:T(8,128)S(1)}, bf16[24,128,128]{2,1,0:T(8,128)(2,1)S(1)}, bf16[64,8,128,128]{3,2,1,0:T(8,128)(2,1)S(1)}) custom-call(s32[16,128]{1,0:T(8,128)S(1)} %get-tuple-element.16.refs_0_.tab_in, bf16[70,128,128]{2,1,0:T(8,128)(2,1)S(1)} %get-tuple-element.17.refs_1_, ...), custom_call_target="tpu_custom_call", output_to_operand_aliasing={{0}: (2, {}), {2}: (3, {})} | custom-call | flops 1500000000 | bytes 8388608 | tf_op jit(solution)/shard_map/phase0/pallas_call | solution.py:396
  16.8 6.5 %collective-permute-start.1 = (bf16[24,128,128]{2,1,0:T(8,128)(2,1)S(1)}, bf16[24,128,128]{2,1,0:T(8,128)(2,1)S(1)}, u32[]{:S(2)}, u32[]{:S(2)}) collective-permute-start(bf16[24,128,128]{2,1,0:T(8,128)(2,1)S(1)} %get-tuple-element.24), channel_id=1, source_target_pairs={{1,0},{2,1},{3,2},{4,3},{5,4},{6,5},{7,6},{8,7},{9,8},{10,9},{11,1... | collective-permute-start | bytes 2359304 | tf_op jit(solution)/shard_map/ppermute | solution.py:479
  23.3 6.9 %phase1.1 = (f32[200,128,128]{2,1,0:T(8,128)S(1)}, bf16[21,128,128]{2,1,0:T(8,128)(2,1)S(1)}) custom-call(s32[16,128]{1,0:T(8,128)S(1)} %get-tuple-element.16.refs_0_.tab_in, bf16[70,128,128]{2,1,0:T(8,128)(2,1)S(1)} %get-tuple-element.17.refs_1_, f32[200,128,128]{2,1,0:T(8,128)S(1)} %get-tuple-element.20.refs_2_, ...), custom_call_target="tpu_custom_call", output_to_operand_aliasing={{0}: (2, {})} | custom-call | flops 1500000000 | bytes 8388608 | tf_op jit(solution)/shard_map/phase1/pallas_call | solution.py:396
  30.3 1.9 %collective-permute-start = (bf16[21,128,128]{2,1,0:T(8,128)(2,1)S(1)}, bf16[21,128,128]{2,1,0:T(8,128)(2,1)S(1)}, u32[]{:S(2)}, u32[]{:S(2)}) collective-permute-start(bf16[21,128,128]{2,1,0:T(8,128)(2,1)S(1)} %get-tuple-element.22), channel_id=1, source_target_pairs={{1,0},{2,1},{3,2},{4,3},{5,4},{6,5},{7,6},{8,7},{9,8},{10,9},{11,1... | collective-permute-start | bytes 2064392 | tf_op jit(solution)/shard_map/ppermute | solution.py:481
  32.2 0.0 collective-permute-done.1.refs_4_
  32.2 7.4 %phase2.1 = (f32[200,128,128]{2,1,0:T(8,128)S(1)}, f32[7,128,128]{2,1,0:T(8,128)S(1)}, f32[16,7,128,128]{3,2,1,0:T(8,128)}) custom-call(s32[16,128]{1,0:T(8,128)S(1)} %get-tuple-element.16.refs_0_.tab_in, bf16[70,128,128]{2,1,0:T(8,128)(2,1)S(1)} %get-tuple-element.17.refs_1_, ...), custom_call_target="tpu_custom_call", output_to_operand_aliasing={{0}: (2, {})} | custom-call | flops 1500000000 | bytes 8388608 | tf_op jit(solution)/shard_map/phase2/pallas_call | solution.py:396
  39.6 2.9 %collective-permute-done.arrived = bf16[21,128,128]{2,1,0:T(8,128)(2,1)S(1)} collective-permute-done((bf16[21,128,128]{2,1,0:T(8,128)(2,1)S(1)}, bf16[21,128,128]{2,1,0:T(8,128)(2,1)S(1)}, u32[]{:S(2)}, u32[]{:S(2)}) %collective-permute-start) | collective-permute-done | bytes 688160 | tf_op jit(solution)/shard_map/ppermute | solution.py:481
  42.5 2.0 %final.1 = f32[16,7,128,128]{3,2,1,0:T(8,128)} custom-call(s32[16,128]{1,0:T(8,128)S(1)} %get-tuple-element.16.refs_0_.tab_in, bf16[21,128,128]{2,1,0:T(8,128)(2,1)S(1)} %collective-permute-done.arrived, f32[7,128,128]{2,1,0:T(8,128)S(1)} %get-tuple-element.25.part, f32[16,7,128,128]{3,2,1,0:T(8,128)} %get-tuple-element.26.out_in), custom_call_target="tpu_custom_call", output_to_operand_aliasing={{}: (3, {})} | custom-call | flops 1000000 | bytes 4194304 | tf_op jit(solution)/shard_map/final/pallas_call | solution.py:454
Async XLA Ops:
  16.8 15.4 %collective-permute-start.1 = (bf16[24,128,128]{2,1,0:T(8,128)(2,1)S(1)}, bf16[24,128,128]{2,1,0:T(8,128)(2,1)S(1)}, u32[]{:S(2)}, u32[]{:S(2)}) collective-permute-start(bf16[24,128,128]{2,1,0:T(8,128)(2,1)S(1)} %get-tuple-element.24), channel_id=1, source_target_pairs={{1,0},{2,1},{3,2},{4,3},{5,4},{6,5},{7,6},{8,7},{9,8},{10,9},{11,1... | collective-permute-start | bytes 2359304 | tf_op jit(solution)/shard_map/ppermute | solution.py:479
  30.3 12.3 %collective-permute-start = (bf16[21,128,128]{2,1,0:T(8,128)(2,1)S(1)}, bf16[21,128,128]{2,1,0:T(8,128)(2,1)S(1)}, u32[]{:S(2)}, u32[]{:S(2)}) collective-permute-start(bf16[21,128,128]{2,1,0:T(8,128)(2,1)S(1)} %get-tuple-element.22), channel_id=1, source_target_pairs={{1,0},{2,1},{3,2},{4,3},{5,4},{6,5},{7,6},{8,7},{9,8},{10,9},{11,1... | collective-permute-start | bytes 2064392 | tf_op jit(solution)/shard_map/ppermute | solution.py:481
where the time goes:
time: 44.7 us; the launch traced here: 44.5 us
  Pallas kernels  33.1 us (74%)
  starting transfers between devices  8.38 us (19%)
  waiting for transfers between devices  2.95 us (7%)
    pallas_call x3, Pallas kernels, phase_call(): pl.pallas_call(functools.partial(phase_kernel, phase), out_shape=shapes,...  20.4 us
    pallas_call x1, Pallas kernels, edges_call(): pl.pallas_call(edges_kernel, out_shape=[jax.ShapeDtypeStruct((RB, K, B, B...  10.7 us
    ppermute x1, starting transfers between devices, shards(): recv_b = lax.ppermute(pack_b, axes, down)  6.46 us
    ppermute x1, waiting for transfers between devices, shards(): recv_a = lax.ppermute(pack_a, axes, down)  2.95 us
    pallas_call x1, Pallas kernels, final_call(): pl.pallas_call(final_kernel, out_shape=jax.ShapeDtypeStruct((AD, KC, B, B...  2.01 us
    ppermute x1, starting transfers between devices, shards(): recv_a = lax.ppermute(pack_a, axes, down)  1.92 us
  transfers between devices with their start and end apart: 2, of which 1 were waited for; matrix products, arithmetic and copies ran while one was open for 0% of the time, Pallas kernels for 32%

commit v1 on v0

--- a/solution.py
+++ b/solution.py
@@ -16,8 +16,9 @@
 B = 128
 RB = 64
 CHUNKS = (21, 24)
-LAST_ROW = 24
-FIRST_ROWS = 20
+LAST_ROW = 28
+FIRST_ROWS = 16
+SECOND_ROWS = 26
 GROUP = 4
 PAD = 7
 OWN = AD * KC
@@ -41,7 +42,8 @@
 T_PHASE = K + 2
 T_RECV = K + 3
 TABLE = (16, 128)
-EARLY = 48
+EARLY = 32
+PIECE = 4
 VMEM_LIMIT = 8 << 20
 
 
@@ -125,11 +127,11 @@
     frame = Frame(starts, dev, devices)
     leaving, cut = frame.chunks()
 
-    own_cut, own_cut_a = frame.boundary(jnp.maximum(frame.shift, FIRST_ROWS))
+    own_cut, _ = frame.boundary(jnp.maximum(frame.shift, FIRST_ROWS))
     r1 = jnp.where(cut >= 0, cut, own_cut)
-    r1_a = jnp.where(cut >= 0, 0, own_cut_a)
-    e1, e1_a = frame.boundary(jnp.maximum(frame.shift, r1 + FIRST_ROWS), EARLY)
-    tab[T_PHASE : T_PHASE + 1] = lanes([r1, e1, r1_a, e1_a, 0, r1, 0, r1_a, e1, RB, e1_a, AD])
+    e1, _ = frame.boundary(jnp.maximum(frame.shift, r1 + FIRST_ROWS), RB - W)
+    e2, e2_a = frame.boundary(e1 + jnp.maximum(SECOND_ROWS - r1, 0), RB - W)
+    tab[T_PHASE : T_PHASE + 1] = lanes([r1, e1, e2, e2_a])
 
     i = lane[:, :RB]
     a = frame.agg(i)
@@ -170,16 +172,21 @@
 
     dev, devices = position(), total()
     cores = lax.axis_size("sub")
+    mesh = pl.DeviceIdType.MESH
 
     def device(d):
-        d = lax.rem(d + devices, devices)
         return (lax.div(d, cores), lax.rem(d, cores))
 
-    left, right = device(dev - 1), device(dev + 1)
-    mesh = pl.DeviceIdType.MESH
+    left, right = device(jnp.maximum(dev - 1, 0)), device(jnp.minimum(dev + 1, devices - 1))
+    has_left, has_right = dev > 0, dev < devices - 1
+    sides = ((has_left, left), (has_right, right))
     barrier = pltpu.get_barrier_semaphore()
-    for other in (left, right):
-        pl.semaphore_signal(barrier, inc=1, device_id=other, device_id_type=mesh)
+    for has, other in sides:
+
+        @pl.when(has)
+        def _(other=other):
+            pl.semaphore_signal(barrier, inc=1, device_id=other, device_id_type=mesh)
+
     for copy in small + local:
         copy.start()
 
@@ -187,7 +194,8 @@
         copy.wait()
     fill_table(starts, offs, counts, tab)
 
-    pl.semaphore_wait(barrier, 2)
+    neighbours = has_left.astype(jnp.int32) + has_right.astype(jnp.int32)
+    pl.semaphore_wait(barrier, neighbours)
     copies = [
         pltpu.make_async_remote_copy(
             src_ref=p_hbm.at[pl.ds(src, W)],
@@ -197,10 +205,10 @@
             device_id=other,
             device_id_type=mesh,
         )
-        for n, src, dst, other in ((0, RB - W, 0, right), (1, 0, RB + W, left))
+        for n, src, dst, other in ((0, 0, RB + W, left), (1, RB - W, 0, right))
     ]
-    for copy in copies:
-        copy.start()
+    for (has, _), copy in zip(sides, copies):
+        pl.when(has)(copy.start)
 
     def clear(b, carry):
         for n in range(CLEAR):
@@ -208,8 +216,16 @@
         return carry
 
     lax.fori_loop(0, BLOCKS // CLEAR, clear, 0)
-    for copy in local + copies:
+    for copy in local:
         copy.wait()
+    for (has, _), copy, at, arrival in zip(sides, copies, (0, RB + W), copies[::-1]):
+        pl.when(has)(copy.wait_send)
+        pl.when(has)(arrival.wait_recv)
+
+        @pl.when(jnp.logical_not(has))
+        def _(at=at):
+            for n in range(W):
+                win[at + n] = jnp.zeros((B, B), BF)
 
 
 def edges_call(starts, offs, counts, a, p):
@@ -255,25 +271,38 @@
     tab_in, win, state, av = refs[:4]
     del refs[:4]
     a_hbm = refs.pop(0) if phase == 0 else None
-    arrived = refs.pop(0) if phase == 2 else None
     blocks = refs.pop(0)
     extra = refs.pop(0)
     if phase == 0:
         av = refs.pop(0)
     out_hbm = refs.pop(0) if phase == 2 else None
-    tab, acc, tab_sem, out_sems, late_sem = refs
+    tab, *acc, tab_sem, out_sems, late_sems = refs
     del state
-    late = pl.ds(EARLY, RB - EARLY)
+
+    def late_copy(n):
+        rows = pl.ds(EARLY + n * PIECE, PIECE)
+        return pltpu.make_async_copy(a_hbm.at[rows], av.at[rows], late_sems.at[n])
+
+    def late_wait(n, carry):
+        late_copy(n).wait()
+        return carry
+
+    late = (RB - EARLY) // PIECE
     if phase == 0:
-        late_copy = pltpu.make_async_copy(a_hbm.at[late], av.at[late], late_sem)
-        late_copy.start()
+        for n in range(late):
+            late_copy(n).start()
     chunk = (1, 0, None)[phase]
 
     tab_copy = pltpu.make_async_copy(tab_in, tab, tab_sem)
     tab_copy.start()
     tab_copy.wait()
-    lo, hi, alo, ahi = [tab[T_PHASE, 4 * phase + n] for n in range(4)]
-    rows = hi - lo
+    r1, e1, e2, e2_a = [tab[T_PHASE, n] for n in range(4)]
+    rows = (e1 - r1, r1 + e2 - e1, RB - e2)[phase]
+
+    def row_at(t):
+        if phase == 1:
+            return t + jnp.where(t < r1, 0, e1 - r1)
+        return t + (r1, 0, e2)[phase]
 
     def out_copy(a):
         return pltpu.make_async_copy(
@@ -289,26 +318,18 @@
         return carry
 
     if phase == 2:
-        lax.fori_loop(0, alo, put, 0)
-
-        def take(a, carry):
-            which, place, low, n = received(tab, a)
-
-            def one(s, carry):
-                blocks[a * KC + low + s] = arrived[place + s].astype(F32)
-                return carry
-
-            lax.fori_loop(0, jnp.where(which == 1, n, 0), one, 0)
-            return carry
-
-        lax.fori_loop(alo, ahi, take, 0)
+        lax.fori_loop(0, e2_a, put, 0)
 
     def group(g, done):
+        if phase == 0:
+            last = row_at(jnp.minimum(g * GROUP + GROUP, rows))
+            need = lax.div(jnp.maximum(last - EARLY, 0) + (PIECE - 1), PIECE)
+            done = lax.fori_loop(done, need, lambda n, c: late_wait(n, c + 1), done)
         places, firsts, goals = [], [], []
         span = jnp.int32(0)
         for u in range(GROUP):
             t = g * GROUP + u
-            i = lo + jnp.minimum(t, rows - 1)
+            i = row_at(jnp.minimum(t, rows - 1))
             head = tab[T_HEAD, i]
             span = jnp.maximum(span, jnp.bitwise_and(lax.shift_right_logical(head, 4), 15))
             places.append(i)
@@ -319,10 +340,11 @@
             applied = []
             heads = [jnp.minimum(f, KC - slots) for f in firsts]
             for u in range(GROUP):
-                i = places[u]
                 for s in range(slots):
-                    acc[u, heads[u] + s] = jnp.zeros((B, B), F32)
-                for k in range(K):
+                    acc[u][heads[u] + s] = jnp.zeros((B, B), F32)
+            for k in range(K):
+                for u in range(GROUP):
+                    i = places[u]
                     code = tab[k, i]
                     slot = lax.shift_right_logical(code, 8)
                     product = jnp.dot(
@@ -330,10 +352,11 @@
                         win[jnp.bitwise_and(code, 255)],
                         preferred_element_type=F32,
                     )
-                    acc[u, slot] = acc[u, slot] + product
+                    acc[u][slot] = acc[u][slot] + product
+            for u in range(GROUP):
                 applied.append(
                     jnp.concatenate(
-                        [acc[u, heads[u] + s].astype(BF) for s in range(slots)], axis=1
+                        [acc[u][heads[u] + s].astype(BF) for s in range(slots)], axis=1
                     )
                 )
             for u in range(GROUP):
@@ -354,24 +377,25 @@
         if phase < 2:
             return done
         t = (g + 1) * GROUP
-        ahead = lax.shift_right_logical(tab[T_HEAD, lo + jnp.minimum(t, rows - 1)], 8)
-        ready = jnp.where(t < rows, jnp.maximum(ahead, alo), alo)
+        ahead = lax.shift_right_logical(tab[T_HEAD, row_at(jnp.minimum(t, rows - 1))], 8)
+        ready = jnp.where(t < rows, ahead, done)
         return lax.fori_loop(done, jnp.maximum(ready, done), lambda a, c: put(a, c + 1), done)
 
-    done = lax.fori_loop(0, lax.div(rows + (GROUP - 1), GROUP), group, alo)
+    start = (0, 0, e2_a)[phase]
+    done = lax.fori_loop(0, lax.div(rows + (GROUP - 1), GROUP), group, jnp.int32(start))
     if chunk is not None:
         for b in range(CHUNKS[chunk]):
             extra[b] = blocks[BASES[chunk] + b].astype(BF)
         if phase == 0:
-            late_copy.wait()
+            lax.fori_loop(done, late, late_wait, 0)
         return
-    lax.fori_loop(done, ahi, put, 0)
-    part = ahi - 1
+    lax.fori_loop(done, AD, put, 0)
+    part = jnp.int32(AD - 1)
     for a in range(AD - 1, -1, -1):
         part = jnp.where(received(tab, a)[3] > 0, a, part)
     for c in range(KC):
         extra[c] = blocks[part * KC + c]
-    lax.fori_loop(0, ahi, put_wait, 0)
+    lax.fori_loop(0, AD, put_wait, 0)
 
 
 def phase_call(phase, tab, win, blocks, a, more=()):
@@ -384,7 +408,6 @@
     if phase == 2:
         shapes.append(jax.ShapeDtypeStruct((KC, B, B), F32))
         shapes.append(jax.ShapeDtypeStruct((AD, KC, B, B), F32))
-        in_specs.append(vmem)
         out_specs.append(hbm)
     else:
         shapes.append(jax.ShapeDtypeStruct((CHUNKS[1 - phase], B, B), BF))
@@ -400,10 +423,10 @@
         out_specs=out_specs,
         scratch_shapes=[
             pltpu.SMEM(TABLE, jnp.int32),
-            pltpu.VMEM((GROUP, K, B, B), F32),
+            *[pltpu.VMEM((K, B, B), F32)] * GROUP,
             pltpu.SemaphoreType.DMA,
             pltpu.SemaphoreType.DMA((AD,)),
-            pltpu.SemaphoreType.DMA,
+            pltpu.SemaphoreType.DMA(((RB - EARLY) // PIECE,)),
         ],
         input_output_aliases=aliases,
         compiler_params=pltpu.CompilerParams(vmem_limit_bytes=VMEM_LIMIT),
@@ -414,23 +437,21 @@
     )(tab, win, blocks, a, *more)
 
 
-def final_kernel(tab_in, arrived, part, out_in, out_hbm, tab, blocks, sems, tab_sem):
+def final_kernel(tab_in, first, second, part, out_in, out_hbm, tab, blocks, sems, tab_sem):
     del out_in
     tab_copy = pltpu.make_async_copy(tab_in, tab, tab_sem)
     tab_copy.start()
     tab_copy.wait()
 
-    def store(a, place, low, s):
-        at = place + s
-        return pltpu.make_async_copy(blocks.at[at], out_hbm.at[a, low + s], sems.at[at])
+    def store(a, at, slot):
+        return pltpu.make_async_copy(blocks.at[at], out_hbm.at[a, slot], sems.at[at])
 
     def each(act):
         def visit(a, seen):
             which, place, low, n = received(tab, a)
-            n = jnp.where(which == 0, n, 0)
 
             def one(s, carry):
-                act(a, place, low, s, seen)
+                act(a, which, place + s, low + s, seen)
                 return carry
 
             lax.fori_loop(0, n, one, 0)
@@ -438,23 +459,33 @@
 
         lax.fori_loop(0, AD, visit, jnp.int32(0))
 
-    def add(a, place, low, s, seen):
-        value = arrived[place + s].astype(F32)
-        blocks[place + s] = jnp.where(seen == 0, value + part[low + s], value)
-        store(a, place, low, s).start()
+    def add(a, which, place, slot, seen):
+        @pl.when(seen == 0)
+        def _():
+            blocks[place] = first[place].astype(F32) + part[slot]
+
+        @pl.when(jnp.logical_and(seen > 0, which == 0))
+        def _():
+            blocks[place] = first[place].astype(F32)
+
+        @pl.when(which == 1)
+        def _():
+            blocks[CHUNKS[0] + place] = second[place].astype(F32)
+
+        store(a, which * CHUNKS[0] + place, slot).start()
 
     each(add)
-    each(lambda a, place, low, s, seen: store(a, place, low, s).wait())
-
-
-def final_call(tab, arrived, part, out):
+    each(lambda a, which, place, slot, seen: store(a, which * CHUNKS[0] + place, slot).wait())
+
+
+def final_call(tab, first, second, part, out):
     vmem = pl.BlockSpec(memory_space=pltpu.VMEM)
     hbm = pl.BlockSpec(memory_space=pltpu.HBM)
-    size = CHUNKS[0]
+    size = sum(CHUNKS)
     return pl.pallas_call(
         final_kernel,
         out_shape=jax.ShapeDtypeStruct((AD, KC, B, B), F32),
-        in_specs=[vmem, vmem, vmem, hbm],
+        in_specs=[vmem, vmem, vmem, vmem, hbm],
         out_specs=hbm,
         scratch_shapes=[
             pltpu.SMEM(TABLE, jnp.int32),
@@ -462,11 +493,11 @@
             pltpu.SemaphoreType.DMA((size,)),
             pltpu.SemaphoreType.DMA,
         ],
-        input_output_aliases={3: 0},
+        input_output_aliases={4: 0},
         compiler_params=pltpu.CompilerParams(vmem_limit_bytes=VMEM_LIMIT),
         cost_estimate=pl.CostEstimate(flops=1_000_000, bytes_accessed=4 << 20, transcendentals=0),
         name="final",
-    )(tab, arrived, part, out)
+    )(tab, first, second, part, out)
 
 
 def shards(a_blocks, nbr_offset, nbr_count, prolong, owner_start):
@@ -479,8 +510,8 @@
     recv_b = lax.ppermute(pack_b, axes, down)
     blocks, pack_a = phase_call(1, tab, win, blocks, a)
     recv_a = lax.ppermute(pack_a, axes, down)
-    blocks, part, out = phase_call(2, tab, win, blocks, a, (recv_b,))
-    return final_call(tab, recv_a, part, out)
+    blocks, part, out = phase_call(2, tab, win, blocks, a)
+    return final_call(tab, recv_a, recv_b, part, out)
 
 
 def solution(mesh):

time: 44.7 us -> 42.4 us (0.949)
  the two profiles are of different devices: /device:TPU:1 before, /device:TPU:125 now
where the time goes in v1:
time: 42.4 us; the launch traced here: 41.9 us
  Pallas kernels  30.2 us (71%)
  waiting for transfers between devices  7.82 us (18%)
  starting transfers between devices  3.84 us (9%)
    pallas_call x3, Pallas kernels, phase_call(): pl.pallas_call(functools.partial(phase_kernel, phase), out_shape=shapes,...  18.8 us
    pallas_call x1, Pallas kernels, edges_call(): pl.pallas_call(edges_kernel, out_shape=[jax.ShapeDtypeStruct((RB, K, B, B...  8.58 us
    ppermute x1, waiting for transfers between devices, shards(): recv_a = lax.ppermute(pack_a, axes, down)  7.81 us
    pallas_call x1, Pallas kernels, final_call(): pl.pallas_call(final_kernel, out_shape=jax.ShapeDtypeStruct((AD, KC, B, B...  2.91 us
    ppermute x1, starting transfers between devices, shards(): recv_b = lax.ppermute(pack_b, axes, down)  1.92 us
    ppermute x1, starting transfers between devices, shards(): recv_a = lax.ppermute(pack_a, axes, down)  1.92 us
  transfers between devices with their start and end apart: 2, of which 1 were waited for; matrix products, arithmetic and copies ran while one was open for 0% of the time, Pallas kernels for 33%

profile of v1, /device:TPU:125, one launch (start us, length us, event | category | flops | bytes accessed | tf_op | source)
XLA Modules:
  0.0 41.9 jit_solution(9303327928516591073)
XLA Ops:
  0.0 8.6 %edges.1 = (bf16[64,8,128,128]{3,2,1,0:T(8,128)(2,1)S(1)}, bf16[70,128,128]{2,1,0:T(8,128)(2,1)S(1)}, f32[200,128,128]{2,1,0:T(8,128)S(1)}, s32[16,128]{1,0:T(8,128)S(1)}) custom-call(s32[128]{0:T(128)} %starts_hbm.1, s32[8,64]{1,0:T(8,128)} %bitcast.2, s32[1,64]{1,0:T(1,128)} %bitcast.3, bf16[64,8,128,128]{3,2,1,0:T(8,128)(2,1)} %refs_4_.1, ...), custom_call_target="tpu_custom_call" | custom-call | flops 1000 | bytes 20971520 | tf_op jit(solution)/shard_map/edges/pallas_call | solution.py:234
  8.6 4.7 %phase0.1 = (f32[200,128,128]{2,1,0:T(8,128)S(1)}, bf16[24,128,128]{2,1,0:T(8,128)(2,1)S(1)}, bf16[64,8,128,128]{3,2,1,0:T(8,128)(2,1)S(1)}) custom-call(s32[16,128]{1,0:T(8,128)S(1)} %get-tuple-element.16.refs_0_.tab_in, bf16[70,128,128]{2,1,0:T(8,128)(2,1)S(1)} %get-tuple-element.17.refs_1_, ...), custom_call_target="tpu_custom_call", output_to_operand_aliasing={{0}: (2, {}), {2}: (3, {})} | custom-call | flops 1500000000 | bytes 8388608 | tf_op jit(solution)/shard_map/phase0/pallas_call | solution.py:419
  13.3 1.9 %collective-permute-start.1 = (bf16[24,128,128]{2,1,0:T(8,128)(2,1)S(1)}, bf16[24,128,128]{2,1,0:T(8,128)(2,1)S(1)}, u32[]{:S(2)}, u32[]{:S(2)}) collective-permute-start(bf16[24,128,128]{2,1,0:T(8,128)(2,1)S(1)} %get-tuple-element.23), channel_id=1, source_target_pairs={{1,0},{2,1},{3,2},{4,3},{5,4},{6,5},{7,6},{8,7},{9,8},{10,9},{11,1... | collective-permute-start | bytes 2359304 | tf_op jit(solution)/shard_map/ppermute | solution.py:510
  15.2 7.3 %phase1.1 = (f32[200,128,128]{2,1,0:T(8,128)S(1)}, bf16[21,128,128]{2,1,0:T(8,128)(2,1)S(1)}) custom-call(s32[16,128]{1,0:T(8,128)S(1)} %get-tuple-element.16.refs_0_.tab_in, bf16[70,128,128]{2,1,0:T(8,128)(2,1)S(1)} %get-tuple-element.17.refs_1_, f32[200,128,128]{2,1,0:T(8,128)S(1)} %get-tuple-element.20.refs_2_, ...), custom_call_target="tpu_custom_call", output_to_operand_aliasing={{0}: (2, {})} | custom-call | flops 1500000000 | bytes 8388608 | tf_op jit(solution)/shard_map/phase1/pallas_call | solution.py:419
  22.6 1.9 %collective-permute-start = (bf16[21,128,128]{2,1,0:T(8,128)(2,1)S(1)}, bf16[21,128,128]{2,1,0:T(8,128)(2,1)S(1)}, u32[]{:S(2)}, u32[]{:S(2)}) collective-permute-start(bf16[21,128,128]{2,1,0:T(8,128)(2,1)S(1)} %get-tuple-element.22), channel_id=1, source_target_pairs={{1,0},{2,1},{3,2},{4,3},{5,4},{6,5},{7,6},{8,7},{9,8},{10,9},{11,1... | collective-permute-start | bytes 2064392 | tf_op jit(solution)/shard_map/ppermute | solution.py:512
  24.5 6.7 %phase2.1 = (f32[200,128,128]{2,1,0:T(8,128)S(1)}, f32[7,128,128]{2,1,0:T(8,128)S(1)}, f32[16,7,128,128]{3,2,1,0:T(8,128)}) custom-call(s32[16,128]{1,0:T(8,128)S(1)} %get-tuple-element.16.refs_0_.tab_in, bf16[70,128,128]{2,1,0:T(8,128)(2,1)S(1)} %get-tuple-element.17.refs_1_, ...), custom_call_target="tpu_custom_call", output_to_operand_aliasing={{0}: (2, {})} | custom-call | flops 1500000000 | bytes 8388608 | tf_op jit(solution)/shard_map/phase2/pallas_call | solution.py:419
  31.2 7.8 %collective-permute-done.first = bf16[21,128,128]{2,1,0:T(8,128)(2,1)S(1)} collective-permute-done((bf16[21,128,128]{2,1,0:T(8,128)(2,1)S(1)}, bf16[21,128,128]{2,1,0:T(8,128)(2,1)S(1)}, u32[]{:S(2)}, u32[]{:S(2)}) %collective-permute-start) | collective-permute-done | bytes 688160 | tf_op jit(solution)/shard_map/ppermute | solution.py:512
  39.0 0.0 collective-permute-done.1.second
  39.0 2.9 %final.1 = f32[16,7,128,128]{3,2,1,0:T(8,128)} custom-call(s32[16,128]{1,0:T(8,128)S(1)} %get-tuple-element.16.refs_0_.tab_in, bf16[21,128,128]{2,1,0:T(8,128)(2,1)S(1)} %collective-permute-done.first, bf16[24,128,128]{2,1,0:T(8,128)(2,1)S(1)} %collective-permute-done.1.second, ...), custom_call_target="tpu_custom_call", output_to_operand_aliasing={{}: (4, {})} | custom-call | flops 1000000 | bytes 4194304 | tf_op jit(solution)/shard_map/final/pallas_call | solution.py:485
Async XLA Ops:
  13.3 25.7 %collective-permute-start.1 = (bf16[24,128,128]{2,1,0:T(8,128)(2,1)S(1)}, bf16[24,128,128]{2,1,0:T(8,128)(2,1)S(1)}, u32[]{:S(2)}, u32[]{:S(2)}) collective-permute-start(bf16[24,128,128]{2,1,0:T(8,128)(2,1)S(1)} %get-tuple-element.23), channel_id=1, source_target_pairs={{1,0},{2,1},{3,2},{4,3},{5,4},{6,5},{7,6},{8,7},{9,8},{10,9},{11,1... | collective-permute-start | bytes 2359304 | tf_op jit(solution)/shard_map/ppermute | solution.py:510
  22.6 16.5 %collective-permute-start = (bf16[21,128,128]{2,1,0:T(8,128)(2,1)S(1)}, bf16[21,128,128]{2,1,0:T(8,128)(2,1)S(1)}, u32[]{:S(2)}, u32[]{:S(2)}) collective-permute-start(bf16[21,128,128]{2,1,0:T(8,128)(2,1)S(1)} %get-tuple-element.22), channel_id=1, source_target_pairs={{1,0},{2,1},{3,2},{4,3},{5,4},{6,5},{7,6},{8,7},{9,8},{10,9},{11,1... | collective-permute-start | bytes 2064392 | tf_op jit(solution)/shard_map/ppermute | solution.py:512
